TPU v7x, 32 devices: a whole 2x2x4 slice. The times are simulated.
32 devices in a mesh: exp: 8 (over z, x), tp: 4 (over y, core).
Axes of the slice: x: 2, y: 2, z: 4, core: 2. Of those that a mesh axis runs over, the one named last changes fastest.
Arguments:
- tokens: bfloat16 [4096, 2048], P(('exp', 'tp')), may hold values from -6 to 6
- cotangent: bfloat16 [4096, 2048], P(('exp', 'tp')), may hold values from -6 to 6
- attention_gain: float32 [2048], replicated, may hold values from 0.5 to 1.5
- query_weight: bfloat16 [2048, 2048], P(None, 'tp'), may hold values from -0.125 to 0.125
- key_weight: bfloat16 [2048, 2048], P(None, 'tp'), may hold values from -0.125 to 0.125
- value_weight: bfloat16 [2048, 2048], P(None, 'tp'), may hold values from -0.125 to 0.125
- output_weight: bfloat16 [2048, 2048], P('tp'), may hold values from -1 to 1
- query_norm: float32 [2048], P('tp'), may hold values from 0.5 to 1.5
- key_norm: float32 [2048], P('tp'), may hold values from 0.5 to 1.5
- mixture_gain: float32 [2048], replicated, may hold values from 0.5 to 1.5
- router_weight: bfloat16 [2048, 16], replicated, may hold values from -0.0625 to 0.0625
- gate_weight: bfloat16 [16, 2048, 1024], P('exp', None, 'tp'), may hold values from -0.125 to 0.125
- up_weight: bfloat16 [16, 2048, 1024], P('exp', None, 'tp'), may hold values from -0.125 to 0.125
- down_weight: bfloat16 [16, 1024, 2048], P('exp', 'tp'), may hold values from -3 to 3
- routes: int32 [4096, 8], P(('exp', 'tp')), may hold values from 0 to 15, all different within a row
- segments: int32 [8, 512], P('exp'), may hold values from 0 to 3, never falling along the last dimension, each value on 1 to 256 neighbouring positions
Outputs:
- output: bfloat16 [4096, 2048], P(('exp', 'tp'))
- tokens_grad: float32 [4096, 2048], P(('exp', 'tp'))
- attention_gain_grad: float32 [2048], replicated
- query_weight_grad: float32 [2048, 2048], P(None, 'tp')
- key_weight_grad: float32 [2048, 2048], P(None, 'tp')
- value_weight_grad: float32 [2048, 2048], P(None, 'tp')
- output_weight_grad: float32 [2048, 2048], P('tp')
- query_norm_grad: float32 [2048], P('tp')
- key_norm_grad: float32 [2048], P('tp')
- mixture_gain_grad: float32 [2048], replicated
- router_weight_grad: float32 [2048, 16], replicated
- gate_weight_grad: float32 [16, 2048, 1024], P('exp', None, 'tp')
- up_weight_grad: float32 [16, 2048, 1024], P('exp', None, 'tp')
- down_weight_grad: float32 [16, 1024, 2048], P('exp', 'tp')
Inputs may be any that keep to these rules, and one draw needn't show every extreme that they name: `routes`: each token names 8 different experts; every expert is named by some token. `segments`: in each row the ids never fall and start at 0; each of the 4 ids covers 1 to 256 consecutive positions, one exactly 256.
All inputs are finite; a program needn't handle non-finite values.
Results may differ from a plain program's by a relative error of at most 0.025.
Values may be sent and summed in bfloat16 or wider, within the bound.
No kernel may reach another device: no remote copies, remote signals or barrier semaphores. Data moves between devices by JAX's collectives and lax.ppermute only.
A program may use at most 256 MiB of HBM per device.

v0:
```python
import math
import jax
import jax.numpy as jnp
from jax import lax
from jax.sharding import PartitionSpec as P

HD = 128
EPS = 1e-05
HIGH = lax.Precision.HIGHEST


def inverse_rms(values):
    return lax.rsqrt(jnp.mean(values * values, axis=-1, keepdims=True) + EPS)


def norm_backward(grad_normed, normalized_input, factor):
    return factor * (
        grad_normed
        - normalized_input * jnp.mean(grad_normed * normalized_input, axis=-1, keepdims=True)
    )


def contract_rows(first_arg, second_arg):
    return lax.dot_general(
        first_arg, second_arg, (((0,), (0,)), ((), ())), preferred_element_type=jnp.float32
    )


def contract_cols(first_arg, second_arg):
    return lax.dot_general(
        first_arg, second_arg, (((1,), (1,)), ((), ())), preferred_element_type=jnp.float32
    )


def positions_of(segment_row):
    earlier = jnp.sum((segment_row[None, :] < segment_row[:, None]).astype(jnp.int32), axis=1)
    return jnp.arange(segment_row.shape[0], dtype=jnp.int32) - earlier


def rope_tables(positions, head_size):
    half_dim = head_size // 2
    inverse_freq = 10000.0 ** (-2.0 * jnp.arange(half_dim).astype(jnp.float32) / head_size)
    angles = positions.astype(jnp.float32)[:, None] * inverse_freq[None, :]
    return (jnp.cos(angles)[:, None, :], jnp.sin(angles)[:, None, :])


def rotate(values, cos_table, sin_table):
    half_dim = values.shape[-1] // 2
    first_half = values[..., :half_dim]
    second_half = values[..., half_dim:]
    return jnp.concatenate(
        [
            first_half * cos_table - second_half * sin_table,
            second_half * cos_table + first_half * sin_table,
        ],
        axis=-1,
    )


def gather_expert_rows(local_rows):
    return lax.all_gather(local_rows, "tp", axis=1, tiled=True)


def body(
    tokens,
    cotangent,
    attention_gain,
    query_weight,
    key_weight,
    value_weight,
    output_weight,
    query_norm,
    key_norm,
    mixture_gain,
    router_weight,
    gate_weight,
    up_weight,
    down_weight,
    routes,
    segments,
):
    tok_rows, model_width = tokens.shape
    top_count = routes.shape[1]
    experts_all = router_weight.shape[1]
    capacity = tok_rows * top_count * 7 // (8 * experts_all)
    local_width = query_weight.shape[1]
    head_count = local_width // HD
    inv_sqrt = 1.0 / math.sqrt(HD)
    inputs = tokens.astype(jnp.float32)
    scale_one = inverse_rms(inputs)
    normed_one = inputs * scale_one
    attention_in = (normed_one * attention_gain).astype(jnp.bfloat16)
    gathered_rows = lax.all_gather(attention_in, "tp", axis=0, tiled=True)
    row_length = gathered_rows.shape[0]
    queries = jnp.dot(gathered_rows, query_weight, preferred_element_type=jnp.float32).reshape(
        row_length, head_count, HD
    )
    key_rows = jnp.dot(gathered_rows, key_weight, preferred_element_type=jnp.float32).reshape(
        row_length, head_count, HD
    )
    value_rows = (
        jnp.dot(gathered_rows, value_weight, preferred_element_type=jnp.float32)
        .astype(jnp.bfloat16)
        .reshape(row_length, head_count, HD)
    )
    query_gain = query_norm.reshape(head_count, HD)
    key_gain = key_norm.reshape(head_count, HD)
    query_scale = inverse_rms(queries)
    query_hat = queries * query_scale
    key_scale = inverse_rms(key_rows)
    key_hat = key_rows * key_scale
    segment_row = segments[0]
    cos_table, sin_table = rope_tables(positions_of(segment_row), HD)
    query_rot = rotate(query_hat * query_gain, cos_table, sin_table).astype(jnp.bfloat16)
    key_rot = rotate(key_hat * key_gain, cos_table, sin_table).astype(jnp.bfloat16)
    block_rows = min(512, row_length)
    position = jnp.arange(row_length, dtype=jnp.int32)

    def block_scores(first_row):
        scores = (
            jnp.einsum("ihd,jhd->hij", query_rot, key_rot, preferred_element_type=jnp.float32)
            * inv_sqrt
        )
        allowed = (
            segment_row[first_row : first_row + block_rows, None] == segment_row[None, :]
        ) & (position[None, :] <= position[first_row : first_row + block_rows, None])
        return jnp.where(allowed[None], scores, -1e30)

    first_row = 0
    scores = block_scores(first_row)
    row_peak = jnp.max(scores, axis=-1, keepdims=True)
    shifted = jnp.exp(scores - row_peak)
    denominator = jnp.sum(shifted, axis=-1, keepdims=True)
    weights = (shifted / denominator).astype(jnp.bfloat16)
    log_totals = [row_peak + jnp.log(denominator)]
    attended_parts = jnp.einsum(
        "hij,jhd->ihd", weights, value_rows, preferred_element_type=jnp.float32
    ).reshape(block_rows, local_width)
    attended = attended_parts.astype(jnp.bfloat16)
    attention_block = lax.psum_scatter(
        jnp.dot(attended, output_weight, preferred_element_type=jnp.float32).astype(jnp.bfloat16),
        "tp",
        scatter_dimension=0,
        tiled=True,
    ).astype(jnp.float32)
    middle = inputs + attention_block
    scale_two = inverse_rms(middle)
    normed_two = middle * scale_two
    mixture_in = (normed_two * mixture_gain).astype(jnp.bfloat16)
    logits = jnp.dot(mixture_in, router_weight, preferred_element_type=jnp.float32)
    probabilities = jax.nn.softmax(logits, axis=-1)
    expert_ids = jnp.arange(experts_all, dtype=jnp.int32)
    chosen = (routes[:, :, None] == expert_ids[None, None, :]).astype(jnp.float32)
    gate_values = jnp.sum(chosen * probabilities[:, None, :], axis=-1)
    assigned = routes.reshape(-1)
    matches = (assigned[:, None] == expert_ids[None, :]).astype(jnp.int32)
    earlier = jnp.sum(jnp.cumsum(matches, axis=0) * matches, axis=1) - 1
    slot_ids = jnp.where(earlier < capacity, assigned * capacity + earlier, experts_all * capacity)
    assign_count = tok_rows * top_count
    owners = (
        jnp.full((experts_all * capacity + 1,), assign_count, jnp.int32)
        .at[slot_ids]
        .set(jnp.arange(assign_count, dtype=jnp.int32))[:-1]
    )
    source_rows = owners // top_count
    input_pad = jnp.concatenate([mixture_in, jnp.zeros((1, model_width), jnp.bfloat16)], axis=0)
    outgoing = input_pad[source_rows].reshape(experts_all, capacity, model_width)
    arrived = lax.all_to_all(outgoing, "exp", split_axis=0, concat_axis=1, tiled=True)
    expert_in = gather_expert_rows(arrived)
    gate_pre = jnp.einsum(
        "erd,edf->erf", expert_in, gate_weight, preferred_element_type=jnp.float32
    )
    up_pre = jnp.einsum("erd,edf->erf", expert_in, up_weight, preferred_element_type=jnp.float32)
    hidden = (jax.nn.silu(gate_pre) * up_pre).astype(jnp.bfloat16)
    partial_out = jnp.einsum(
        "erf,efd->erd", hidden, down_weight, preferred_element_type=jnp.float32
    )
    returned = lax.psum_scatter(
        partial_out.astype(jnp.bfloat16), "tp", scatter_dimension=1, tiled=True
    )
    combined = lax.all_to_all(returned, "exp", split_axis=1, concat_axis=0, tiled=True)
    output_pad = jnp.concatenate(
        [combined.reshape(-1, model_width), jnp.zeros((1, model_width), jnp.bfloat16)], axis=0
    )
    expert_out = output_pad[slot_ids].astype(jnp.float32).reshape(tok_rows, top_count, model_width)
    mixture = jnp.sum(gate_values[:, :, None] * expert_out, axis=1)
    output = (middle + mixture).astype(jnp.bfloat16)
    grad_out = cotangent.astype(jnp.float32)
    grad_gate = jnp.sum(grad_out[:, None, :] * expert_out, axis=-1)
    grad_sent = (
        (gate_values[:, :, None] * grad_out[:, None, :])
        .reshape(assign_count, model_width)
        .astype(jnp.bfloat16)
    )
    grad_pad = jnp.concatenate([grad_sent, jnp.zeros((1, model_width), jnp.bfloat16)], axis=0)
    grad_outgoing = grad_pad[owners].reshape(experts_all, capacity, model_width)
    grad_arrived = lax.all_to_all(grad_outgoing, "exp", split_axis=0, concat_axis=1, tiled=True)
    grad_expert = lax.all_gather(grad_arrived, "tp", axis=1, tiled=True)
    gate_pre = jnp.einsum(
        "erd,edf->erf", expert_in, gate_weight, preferred_element_type=jnp.float32
    )
    up_pre = jnp.einsum("erd,edf->erf", expert_in, up_weight, preferred_element_type=jnp.float32)
    gate_sig = jax.nn.sigmoid(gate_pre)
    gate_act = gate_pre * gate_sig
    hidden = (gate_act * up_pre).astype(jnp.bfloat16)
    grad_hidden = jnp.einsum(
        "erd,efd->erf", grad_expert, down_weight, preferred_element_type=jnp.float32
    )
    down_grad = jnp.einsum("erf,erd->efd", hidden, grad_expert, preferred_element_type=jnp.float32)
    grad_gate_pre = (grad_hidden * up_pre * gate_sig * (1.0 + gate_pre * (1.0 - gate_sig))).astype(
        jnp.bfloat16
    )
    grad_up_pre = (grad_hidden * gate_act).astype(jnp.bfloat16)
    gate_grad = jnp.einsum(
        "erd,erf->edf", expert_in, grad_gate_pre, preferred_element_type=jnp.float32
    )
    up_grad = jnp.einsum("erd,erf->edf", expert_in, grad_up_pre, preferred_element_type=jnp.float32)
    grad_in_part = jnp.einsum(
        "erf,edf->erd", grad_gate_pre, gate_weight, preferred_element_type=jnp.float32
    ) + jnp.einsum("erf,edf->erd", grad_up_pre, up_weight, preferred_element_type=jnp.float32)
    grad_in = lax.psum_scatter(
        grad_in_part.astype(jnp.bfloat16), "tp", scatter_dimension=1, tiled=True
    )
    grad_home = lax.all_to_all(grad_in, "exp", split_axis=1, concat_axis=0, tiled=True)
    home_pad = jnp.concatenate(
        [grad_home.reshape(-1, model_width), jnp.zeros((1, model_width), jnp.bfloat16)], axis=0
    )
    grad_assigned = home_pad[slot_ids].astype(jnp.float32).reshape(tok_rows, top_count, model_width)
    grad_probs = jnp.sum(chosen * grad_gate[:, :, None], axis=1)
    grad_logits = probabilities * (
        grad_probs - jnp.sum(grad_probs * probabilities, axis=-1, keepdims=True)
    )
    router_grad = jnp.dot(mixture_in.astype(jnp.float32).T, grad_logits, precision=HIGH)
    grad_mixture_in = jnp.sum(grad_assigned, axis=1) + jnp.dot(
        grad_logits, router_weight.astype(jnp.float32).T, precision=HIGH
    )
    mixture_gain_grad = jnp.sum(grad_mixture_in * normed_two, axis=0)
    grad_middle = grad_out + norm_backward(grad_mixture_in * mixture_gain, normed_two, scale_two)
    grad_attention = grad_middle.astype(jnp.bfloat16)
    row_grad = lax.all_gather(grad_attention, "tp", axis=0, tiled=True)
    output_weight_grad = contract_rows(attended, row_grad)
    grad_attended = contract_cols(row_grad, output_weight).astype(jnp.bfloat16)
    grad_query_parts = []
    grad_key_rows = jnp.zeros((row_length, head_count, HD), jnp.float32)
    grad_value_rows = jnp.zeros((row_length, head_count, HD), jnp.float32)
    for block_index, first_row in enumerate(range(0, row_length, block_rows)):
        scores = block_scores(first_row)
        probs_block = jnp.exp(scores - log_totals[block_index])
        weights = probs_block.astype(jnp.bfloat16)
        grad_block = grad_attended.reshape(block_rows, head_count, HD)
        grad_weights = jnp.einsum(
            "ihd,jhd->hij", grad_block, value_rows, preferred_element_type=jnp.float32
        )
        inner_sum = jnp.sum(grad_weights * probs_block, axis=-1, keepdims=True)
        grad_scores = (probs_block * (grad_weights - inner_sum)).astype(jnp.bfloat16)
        grad_query_parts.append(
            jnp.einsum("hij,jhd->ihd", grad_scores, key_rot, preferred_element_type=jnp.float32)
            * inv_sqrt
        )
        grad_key_rows = (
            jnp.einsum("hij,ihd->jhd", grad_scores, query_rot, preferred_element_type=jnp.float32)
            * inv_sqrt
        )
        grad_value_rows = jnp.einsum(
            "hij,ihd->jhd", weights, grad_block, preferred_element_type=jnp.float32
        )
    grad_query_norm = rotate(grad_query_parts[0], cos_table, -sin_table)
    grad_key_norm = rotate(grad_key_rows, cos_table, -sin_table)
    query_norm_grad = jnp.sum(grad_query_norm * query_hat, axis=0).reshape(local_width)
    key_norm_grad = jnp.sum(grad_key_norm * key_hat, axis=0).reshape(local_width)
    grad_queries = (
        norm_backward(grad_query_norm * query_gain, query_hat, query_scale)
        .reshape(row_length, local_width)
        .astype(jnp.bfloat16)
    )
    grad_keys = (
        norm_backward(grad_key_norm * key_gain, key_hat, key_scale)
        .reshape(row_length, local_width)
        .astype(jnp.bfloat16)
    )
    grad_values = grad_value_rows.reshape(row_length, local_width).astype(jnp.bfloat16)
    query_weight_grad = contract_rows(gathered_rows, grad_queries)
    key_weight_grad = contract_rows(gathered_rows, grad_keys)
    value_weight_grad = contract_rows(gathered_rows, grad_values)
    total_grad = contract_cols(grad_queries, query_weight)
    total_grad = total_grad + contract_cols(grad_keys, key_weight)
    grad_attention_in = lax.psum_scatter(
        (total_grad + contract_cols(grad_values, value_weight)).astype(jnp.bfloat16),
        "tp",
        scatter_dimension=0,
        tiled=True,
    ).astype(jnp.float32)
    attention_gain_grad = jnp.sum(grad_attention_in * normed_one, axis=0)
    tokens_grad = grad_middle + norm_backward(
        grad_attention_in * attention_gain, normed_one, scale_one
    )
    head_sums = (
        lax.psum(query_weight_grad.astype(jnp.bfloat16), "exp").astype(jnp.float32),
        lax.psum(key_weight_grad.astype(jnp.bfloat16), "exp").astype(jnp.float32),
        lax.psum(value_weight_grad.astype(jnp.bfloat16), "exp").astype(jnp.float32),
        lax.psum(output_weight_grad.astype(jnp.bfloat16), "exp").astype(jnp.float32),
        lax.psum(query_norm_grad.astype(jnp.bfloat16), "exp").astype(jnp.float32),
        lax.psum(key_norm_grad.astype(jnp.bfloat16), "exp").astype(jnp.float32),
    )
    shared_sums = lax.psum((attention_gain_grad, mixture_gain_grad, router_grad), ("exp", "tp"))
    return (
        output,
        tokens_grad,
        shared_sums[0],
        head_sums[0],
        head_sums[1],
        head_sums[2],
        head_sums[3],
        head_sums[4],
        head_sums[5],
        shared_sums[1],
        shared_sums[2],
        gate_grad,
        up_grad,
        down_grad,
    )


def solution(mesh):
    return jax.shard_map(
        body,
        mesh=mesh,
        in_specs=(
            P(("exp", "tp"), None),
            P(("exp", "tp"), None),
            P(),
            P(None, "tp"),
            P(None, "tp"),
            P(None, "tp"),
            P("tp", None),
            P("tp"),
            P("tp"),
            P(),
            P(),
            P("exp", None, "tp"),
            P("exp", None, "tp"),
            P("exp", "tp", None),
            P(("exp", "tp"), None),
            P("exp", None),
        ),
        out_specs=(
            P(("exp", "tp"), None),
            P(("exp", "tp"), None),
            P(),
            P(None, "tp"),
            P(None, "tp"),
            P(None, "tp"),
            P("tp", None),
            P("tp"),
            P("tp"),
            P(),
            P(),
            P("exp", None, "tp"),
            P("exp", None, "tp"),
            P("exp", "tp", None),
        ),
        check_vma=False,
    )
```

profile of v0, /device:TPU:0, one launch (start us, length us, event | category | flops | bytes accessed | tf_op | source)
XLA Modules:
  0.0 1259.1 jit_solution(2690776216427497176)
XLA Ops:
  15.7 21.0 %all-gather.5.cloned.1.call-done = bf16[512,2048]{1,0:T(8,128)(2,1)} async-done(((bf16[128,2048]{1,0:T(8,128)(2,1)}), bf16[512,2048]{1,0:T(8,128)(2,1)}) %all-gather.5.cloned.1.call-update) | async-done | bytes 2097168 | tf_op jit(solution)/shard_map/all_gather | solution.py:93
  71.9 21.5 %reduce-scatter.5.cloned.1.call-done = bf16[128,2048]{1,0:T(8,128)(2,1)} async-done(((bf16[512,2048]{1,0:T(8,128)(2,1)}), bf16[128,2048]{1,0:T(8,128)(2,1)}) %reduce-scatter.5.cloned.1.call-update) | async-done | bytes 524304 | tf_op jit(solution)/shard_map/reduce_scatter | solution.py:140
  101.7 87.5 %all_to_all.66 = bf16[16,56,2048]{2,1,0:T(8,128)(2,1)S(1)} all-to-all(bf16[16,56,2048]{2,1,0:T(8,128)(2,1)} %bitcast.163), channel_id=1, replica_groups=mesh['exp'=8,'tp'=4] {'exp'}, dimensions={0} | all-to-all | bytes 7340032 | tf_op jit(solution)/shard_map/all_to_all | solution.py:168
  197.7 12.3 gather_fusion.2
  210.0 85.0 %all_to_all.67 = bf16[16,56,2048]{2,1,0:T(8,128)(2,1)S(1)} all-to-all(bf16[16,56,2048]{2,1,0:T(8,128)(2,1)} %bitcast.164), channel_id=1, replica_groups=mesh['exp'=8,'tp'=4] {'exp'}, dimensions={0} | all-to-all | bytes 7340032 | tf_op jit(solution)/shard_map/all_to_all | solution.py:197
  297.5 13.5 %fusion.53 = f32[2,1792,256]{2,1,0:T(8,128)} fusion(bf16[2,1792,2048]{2,1,0:T(8,128)(2,1)} %all-gather.7.cloned.1.call-done, bf16[2,2048,256]{2,1,0:T(8,128)(2,1)} %param.28), kind=kOutput, calls=%fused_computation.159 | convolution fusion | flops 3758096384 | bytes 20447232 | tf_op jit(solution)/shard_map/erd,edf->erf/dot_general | solution.py:173
  310.9 9.8 fusion.52
  320.8 68.7 %all-gather.9.cloned.1.call-done = bf16[2,1792,2048]{2,1,0:T(8,128)(2,1)} async-done(((bf16[2,448,2048]{2,1,0:T(8,128)(2,1)}), bf16[2,1792,2048]{2,1,0:T(8,128)(2,1)}) %all-gather.9.cloned.1.call-update) | async-done | bytes 14680080 | tf_op jit(solution)/shard_map/all_gather | solution.py:198
  389.5 15.6 %multiply_convert_fusion.1 = (bf16[2,1792,256]{2,1,0:T(8,128)(2,1)}, bf16[2,1792,256]{2,1,0:T(8,128)(2,1)}, bf16[2,1792,256]{2,1,0:T(8,128)(2,1)}) fusion(f32[2,1792,256]{2,1,0:T(8,128)} %fusion.52, f32[2,1792,256]{2,1,0:T(8,128)} %fusion.53, bf16[2,1792,2048]{2,1,0:T(8,128)(2,1)} %all-gather.9.cloned.1.call-done, bf16[2,256,2048]{2,1,0:T(8,128)(2,1)S(1)} %copy-done), kind=kOutput, calls=%fused_computation.22 | convolution fusion | flops 3771858944 | bytes 29622272 | tf_op jit(solution)/shard_map/erd,efd->erf/dot_general | solution.py:206
  405.0 8.7 convolution_convert_fusion
  415.3 19.2 %fusion.54 = f32[2,1792,2048]{2,1,0:T(8,128)} fusion(bf16[2,1792,256]{2,1,0:T(8,128)(2,1)} %get-tuple-element.33, bf16[2,2048,256]{2,1,0:T(8,128)(2,1)S(1)} %copy-done.34), kind=kOutput, calls=%fused_computation.160 | convolution fusion | flops 3758096384 | bytes 33292288 | tf_op jit(solution)/shard_map/erf,edf->erd/dot_general | solution.py:218
  434.6 17.7 %add_convert_fusion = bf16[2,1792,2048]{2,1,0:T(8,128)(2,1)} fusion(f32[2,1792,2048]{2,1,0:T(8,128)} %fusion.54, bf16[2,1792,256]{2,1,0:T(8,128)(2,1)S(1)} %copy-done.43, bf16[2,2048,256]{2,1,0:T(8,128)(2,1)S(1)} %copy-done.35), kind=kOutput, calls=%fused_computation.5 | convolution fusion | flops 3772776448 | bytes 47972352 | tf_op jit(solution)/shard_map/erf,edf->erd/dot_general | solution.py:220
  452.3 74.5 %reduce-scatter.7.cloned.1.call-done = bf16[2,448,2048]{2,1,0:T(8,128)(2,1)} async-done(((bf16[2,1792,2048]{2,1,0:T(8,128)(2,1)}), bf16[2,448,2048]{2,1,0:T(8,128)(2,1)}) %reduce-scatter.7.cloned.1.call-update) | async-done | bytes 3670032 | tf_op jit(solution)/shard_map/reduce_scatter | solution.py:178
  539.9 102.3 %reduce-scatter.9.cloned.1.call-done = bf16[2,448,2048]{2,1,0:T(8,128)(2,1)} async-done(((bf16[2,1792,2048]{2,1,0:T(8,128)(2,1)}), bf16[2,448,2048]{2,1,0:T(8,128)(2,1)}) %reduce-scatter.9.cloned.1.call-update) | async-done | bytes 3670032 | tf_op jit(solution)/shard_map/reduce_scatter | solution.py:221
  661.9 11.3 gather_fusion.1
  679.2 58.3 %all-to-all-done.3 = bf16[2,448,2048]{2,0,1:T(2,128)(2,1)} async-done(((bf16[2,448,2048]{2,0,1:T(2,128)(2,1)}), bf16[2,448,2048]{2,0,1:T(2,128)(2,1)}, u32[]{:S(2)}, u32[]{:S(2)}) %all-to-all-start.3) | async-done | bytes 3670048 | tf_op jit(solution)/shard_map/all_to_all | solution.py:224
  743.4 11.3 gather_fusion.3
  762.6 20.6 %all-gather.11.cloned.1.call-done = bf16[512,2048]{1,0:T(8,128)(2,1)} async-done(((bf16[128,2048]{1,0:T(8,128)(2,1)}), bf16[512,2048]{1,0:T(8,128)(2,1)}) %all-gather.11.cloned.1.call-update) | async-done | bytes 2097168 | tf_op jit(solution)/shard_map/all_gather | solution.py:240
  824.9 11.0 fusion.58
  835.9 11.0 fusion.57
  853.7 22.3 %all-reduce.5 = (bf16[512]{0:T(512)(128)(2,1)S(1)}, bf16[512]{0:T(512)(128)(2,1)S(1)}) all-reduce(bf16[512]{0:T(512)(128)(2,1)S(1)} %get-tuple-element.37, bf16[512]{0:T(512)(128)(2,1)S(1)} %get-tuple-element.35), channel_id=1, replica_groups=mesh['exp'=8,'tp'=4] {'exp'}, use_global_device_ids=true, to_apply=%region_35.36 | all-reduce | flops 1024 | bytes 4096 | tf_op jit(solution)/shard_map/psum | solution.py:302
  882.0 40.7 %all-reduce.4 = (f32[2048]{0:T(1024)}, f32[2048]{0:T(1024)}) all-reduce(f32[2048]{0:T(1024)S(1)} %get-tuple-element.18, f32[2048]{0:T(1024)S(1)} %get-tuple-element.16), channel_id=1, replica_groups=mesh['exp'=8,'tp'=4] {'exp','tp'}, use_global_device_ids=true, to_apply=%region_29.30 | all-reduce | flops 4096 | bytes 32768 | tf_op jit(solution)/shard_map/psum | solution.py:305
  922.7 200.3 %all-reduce.12.cloned.1.call-done = (bf16[2048,512]{1,0:T(8,128)(2,1)}, bf16[2048,512]{1,0:T(8,128)(2,1)}, bf16[2048,512]{1,0:T(8,128)(2,1)}, bf16[512,2048]{1,0:T(8,128)(2,1)}) async-done(((bf16[2048,512]{1,0:T(8,128)(2,1)}, bf16[2048,512]{1,0:T(8,128)(2,1)}, bf16[2048,512]{1,0:T(8,128)(2,1)}, bf16[512,2048]{1,0:T(8,128)(2,1)}), (bf16[2048,512]{1,0:T(8,128)(2,1)}, bf16[2048,512]{1,0:T(8,128)(2,1)}, ...) | async-done | bytes 8388624 | tf_op jit(solution)/shard_map/psum | solution.py:298
  1135.3 115.1 %all-reduce.10.cloned.1.call-done = f32[2048,16]{0,1:T(8,128)} async-done(((f32[2048,16]{0,1:T(8,128)}), f32[2048,16]{0,1:T(8,128)}) %all-reduce.10.cloned.1.call-update) | async-done | bytes 131088 | tf_op jit(solution)/shard_map/psum | solution.py:305
  (293 shorter events, 184.2 us)
Async XLA Ops:
  7.2 382.3 %copy-start = (bf16[2,256,2048]{2,1,0:T(8,128)(2,1)S(1)}, bf16[2,256,2048]{2,1,0:T(8,128)(2,1)}, u32[]{:S(2)}) copy-start(bf16[2,256,2048]{2,1,0:T(8,128)(2,1)} %param.29) | copy-start | bytes 6291460
  7.2 29.5 %all-gather.5.cloned.1.call-start = ((), (), s32[]{:S(2)}) async-start(), calls=%async_computation.8 | async-start | bytes 2621440 | tf_op jit(solution)/shard_map/all_gather | solution.py:93
  11.2 82.1 %reduce-scatter.5.cloned.1.call-start = ((), (), s32[]{:S(2)}) async-start(), calls=%async_computation.9 | async-start | bytes 2621440 | tf_op jit(solution)/shard_map/reduce_scatter | solution.py:140
  15.7 34.2 %copy-start.31 = (f32[512,64]{1,0:T(8,128)}, f32[512,64]{1,0:T(8,128)S(1)}, u32[]{:S(2)}) copy-start(f32[512,64]{1,0:T(8,128)S(1)} %get-tuple-element.57) | copy-start | bytes 393220
  59.1 34.3 %copy-start.4 = (bf16[128,2048]{1,0:T(8,128)(2,1)S(1)}, bf16[128,2048]{1,0:T(8,128)(2,1)}, u32[]{:S(2)}) copy-start(bf16[128,2048]{1,0:T(8,128)(2,1)} %param.16) | copy-start | bytes 1572868
  59.1 35.6 %copy-start.50 = (f32[2048]{0:T(1024)S(1)}, f32[2048]{0:T(1024)}, u32[]{:S(2)}) copy-start(f32[2048]{0:T(1024)} %param.25) | copy-start | bytes 24580
  61.7 235.7 %all-gather.7.cloned.1.call-start = ((), (), s32[]{:S(2)}) async-start(), calls=%async_computation.10 | async-start | bytes 18350080 | tf_op jit(solution)/shard_map/all_gather | solution.py:61
  191.5 197.9 %all-gather.9.cloned.1.call-start = ((), (), s32[]{:S(2)}) async-start(), calls=%async_computation.12 | async-start | bytes 18350080 | tf_op jit(solution)/shard_map/all_gather | solution.py:198
  297.4 229.4 %reduce-scatter.7.cloned.1.call-start = ((), (), s32[]{:S(2)}) async-start(), calls=%async_computation.11 | async-start | bytes 18350080 | tf_op jit(solution)/shard_map/reduce_scatter | solution.py:178
  413.8 228.5 %reduce-scatter.9.cloned.1.call-start = ((), (), s32[]{:S(2)}) async-start(), calls=%async_computation.13 | async-start | bytes 18350080 | tf_op jit(solution)/shard_map/reduce_scatter | solution.py:221
  415.3 19.2 %copy-start.35 = (bf16[2,2048,256]{2,1,0:T(8,128)(2,1)S(1)}, bf16[2,2048,256]{2,1,0:T(8,128)(2,1)}, u32[]{:S(2)}) copy-start(bf16[2,2048,256]{2,1,0:T(8,128)(2,1)} %param.28) | copy-start | bytes 6291460
  415.3 19.2 %copy-start.43 = (bf16[2,1792,256]{2,1,0:T(8,128)(2,1)S(1)}, bf16[2,1792,256]{2,1,0:T(8,128)(2,1)}, u32[]{:S(2)}) copy-start(bf16[2,1792,256]{2,1,0:T(8,128)(2,1)} %get-tuple-element.32) | copy-start | bytes 5505028
  534.4 115.5 %all-to-all-start.1 = ((bf16[2,448,2048]{2,0,1:T(2,128)(2,1)}), bf16[2,448,2048]{2,0,1:T(2,128)(2,1)}, u32[]{:S(2)}, u32[]{:S(2)}) async-start(bf16[2,448,2048]{2,0,1:T(2,128)(2,1)} %copy.151), calls=%async_computation.3 | async-start | bytes 7340032 | tf_op jit(solution)/shard_map/all_to_all | solution.py:181
  649.9 87.6 %all-to-all-start.3 = ((bf16[2,448,2048]{2,0,1:T(2,128)(2,1)}), bf16[2,448,2048]{2,0,1:T(2,128)(2,1)}, u32[]{:S(2)}, u32[]{:S(2)}) async-start(bf16[2,448,2048]{2,0,1:T(2,128)(2,1)} %copy.155), calls=%async_computation.6 | async-start | bytes 7340032 | tf_op jit(solution)/shard_map/all_to_all | solution.py:224
  655.4 127.8 %all-gather.11.cloned.1.call-start = ((), (), s32[]{:S(2)}) async-start(), calls=%async_computation.14 | async-start | bytes 2621440 | tf_op jit(solution)/shard_map/all_gather | solution.py:240
  762.3 114.9 %reduce-scatter.11.cloned.1.call-start = ((), (), s32[]{:S(2)}) async-start(), calls=%async_computation.15 | async-start | bytes 2621440 | tf_op jit(solution)/shard_map/reduce_scatter | solution.py:287
  812.4 310.6 %all-reduce.12.cloned.1.call-start = ((), (), s32[]{:S(2)}) async-start(), calls=%async_computation.17 | async-start | bytes 16777216 | tf_op jit(solution)/shard_map/psum | solution.py:298
  824.8 425.5 %all-reduce.10.cloned.1.call-start = ((), (), s32[]{:S(2)}) async-start(), calls=%async_computation.16 | async-start | bytes 262144 | tf_op jit(solution)/shard_map/psum | solution.py:305
  824.9 22.0 %slice-start = ((s8[14680064]{0:T(1024)(128)(4,1)}), s8[4194304]{0:T(1024)(128)(4,1)S(1)}, s32[]{:S(2)}) async-start(s8[14680064]{0:T(1024)(128)(4,1)} %bitcast.161), calls=%async_computation.18 | async-start | bytes 8388608
  824.9 22.0 %slice-start.1 = ((s8[14680064]{0:T(1024)(128)(4,1)}), s8[4194304]{0:T(1024)(128)(4,1)S(1)}, s32[]{:S(2)}) async-start(s8[14680064]{0:T(1024)(128)(4,1)} %bitcast.161), calls=%async_computation.19 | async-start | bytes 8388608
  847.0 30.2 %copy-start.56 = (f32[2048]{0:T(1024)S(1)}, f32[2048]{0:T(1024)}, u32[]{:S(2)}) copy-start(f32[2048]{0:T(1024)} %param.18) | copy-start | bytes 24580
  847.0 30.2 %copy-start.69 = (f32[128]{0:T(128)S(1)}, f32[128]{0:T(128)}, u32[]{:S(2)}) copy-start(f32[128]{0:T(128)} %copy-done.68) | copy-start | bytes 1540
  847.0 31.7 %copy-start.14 = (bf16[128,2048]{1,0:T(8,128)(2,1)S(1)}, bf16[128,2048]{1,0:T(8,128)(2,1)}, u32[]{:S(2)}) copy-start(bf16[128,2048]{1,0:T(8,128)(2,1)} %param.17) | copy-start | bytes 1572868
  1130.0 121.9 %copy-start.1 = (bf16[2,256,2048]{2,1,0:T(8,128)(2,1)S(1)}, bf16[2,256,2048]{2,1,0:T(8,128)(2,1)}, u32[]{:S(2)}) copy-start(bf16[2,256,2048]{2,1,0:T(8,128)(2,1)} %param.29) | copy-start | bytes 6291460
  (67 other events, 237.3 us)
Sparse Core Ops, SparseCore 0:
  11.4 25.2 all-gather.4
  61.8 31.4 reduce-scatter.4
  191.6 92.0 all-gather.6
  297.5 91.9 all-gather.8
  413.9 112.8 reduce-scatter.6
  529.4 112.8 reduce-scatter.8
  762.4 20.6 all-gather.10
  812.5 31.4 reduce-scatter.10
  849.2 273.8 all-reduce.11
  1129.0 121.2 all-reduce.9
where the time goes:
time: 1270 us; the launch traced here: 1260 us
  waiting for transfers between devices  682 us (54%)
  blocking collectives  236 us (19%)
  matrix products  157 us (12%)
  local copies, waits for them, and re-layouts  97.1 us (8%)
  other arithmetic  58.7 us (5%)
  between operations  15.7 us (1%)
    psum x1, waiting for transfers between devices, body(): lax.psum(query_weight_grad.astype(jnp.bfloat16), 'exp').astype(jnp.float32)  200 us
    psum x1, waiting for transfers between devices, body(): lax.psum((attention_gain_grad, mixture_gain_grad, router_grad), ('exp', '...  115 us
    reduce_scatter x1, waiting for transfers between devices, body(): lax.psum_scatter(grad_in_part.astype(jnp.bfloat16), 'tp', scatter_dimensi...  102 us
    all_to_all x1, blocking collectives, body(): lax.all_to_all(outgoing, 'exp', split_axis=0, concat_axis=1, tiled=True)  87.5 us
    all_to_all x1, blocking collectives, body(): lax.all_to_all(grad_outgoing, 'exp', split_axis=0, concat_axis=1, tiled=T...  85 us
    reduce_scatter x1, waiting for transfers between devices, body(): lax.psum_scatter(partial_out.astype(jnp.bfloat16), 'tp', scatter_dimensio...  74.5 us
    all_gather x1, waiting for transfers between devices, body(): grad_expert = lax.all_gather(grad_arrived, 'tp', axis=1, tiled=True)  68.7 us
    all_to_all x1, waiting for transfers between devices, body(): lax.all_to_all(grad_in, 'exp', split_axis=1, concat_axis=0, tiled=True)  58.3 us
  transfers between devices with their start and end apart: 12, of which 9 were waited for; matrix products, arithmetic and copies ran while one was open for 15% of the time, Pallas kernels for 0%

commit v1 on v0

--- a/solution.py
+++ b/solution.py
@@ -1,12 +1,21 @@
+import functools
 import math
 import jax
 import jax.numpy as jnp
 from jax import lax
 from jax.sharding import PartitionSpec as P
+from jax.lax import all_gather
 
 HD = 128
 EPS = 1e-05
 HIGH = lax.Precision.HIGHEST
+
+
+def wait_orders(content, named_axis):
+    return all_gather(content, named_axis).sum(axis=0)
+
+
+expand_numbers = functools.partial(wait_orders, named_axis="exp")
 
 
 def inverse_rms(values):
@@ -295,7 +304,7 @@
         grad_attention_in * attention_gain, normed_one, scale_one
     )
     head_sums = (
-        lax.psum(query_weight_grad.astype(jnp.bfloat16), "exp").astype(jnp.float32),
+        expand_numbers(query_weight_grad.astype(jnp.bfloat16)).astype(jnp.float32),
         lax.psum(key_weight_grad.astype(jnp.bfloat16), "exp").astype(jnp.float32),
         lax.psum(value_weight_grad.astype(jnp.bfloat16), "exp").astype(jnp.float32),
         lax.psum(output_weight_grad.astype(jnp.bfloat16), "exp").astype(jnp.float32),

time: 1270 us -> 1440 us (1.13)
  waiting for transfers between devices: 682 us -> 837 us
    all_gather x0 -> x1, waiting for transfers between devices: none -> 220 us  [wait_orders(): return all_gather(content, named_axis).sum(axis=0)]
    psum x1, waiting for transfers between devices: 200 us -> 138 us  [body(): lax.psum(key_weight_grad.astype(jnp.bfloat16), 'exp').astype(jnp.float32)]
  transfers between devices with their start and end apart: 12 -> 13, of which waited for: 9 -> 10; matrix products, arithmetic and copies ran while one was open for 15% -> 14% of each run, Pallas kernels for 0% -> 0%
where the time goes in v1:
time: 1440 us; the launch traced here: 1430 us
  waiting for transfers between devices  837 us (58%)
  blocking collectives  235 us (16%)
  matrix products  159 us (11%)
  local copies, waits for them, and re-layouts  98.1 us (7%)
  other arithmetic  70.9 us (5%)
  between operations  15.4 us (1%)
    all_gather x1, waiting for transfers between devices, wait_orders(): return all_gather(content, named_axis).sum(axis=0)  220 us
    psum x1, waiting for transfers between devices, body(): lax.psum(key_weight_grad.astype(jnp.bfloat16), 'exp').astype(jnp.float32)  138 us
    psum x1, waiting for transfers between devices, body(): lax.psum((attention_gain_grad, mixture_gain_grad, router_grad), ('exp', '...  113 us
    reduce_scatter x1, waiting for transfers between devices, body(): lax.psum_scatter(grad_in_part.astype(jnp.bfloat16), 'tp', scatter_dimensi...  102 us
    all_to_all x1, blocking collectives, body(): lax.all_to_all(outgoing, 'exp', split_axis=0, concat_axis=1, tiled=True)  87.5 us
    all_to_all x1, blocking collectives, body(): lax.all_to_all(grad_outgoing, 'exp', split_axis=0, concat_axis=1, tiled=T...  85 us
    reduce_scatter x1, waiting for transfers between devices, body(): lax.psum_scatter(partial_out.astype(jnp.bfloat16), 'tp', scatter_dimensio...  74.5 us
    all_gather x1, waiting for transfers between devices, body(): grad_expert = lax.all_gather(grad_arrived, 'tp', axis=1, tiled=True)  68.7 us
  transfers between devices with their start and end apart: 13, of which 10 were waited for; matrix products, arithmetic and copies ran while one was open for 14% of the time, Pallas kernels for 0%

profile of v1, /device:TPU:0, one launch (start us, length us, event | category | flops | bytes accessed | tf_op | source)
XLA Modules:
  0.0 1429.0 jit_solution(8788435941878631585)
XLA Ops:
  15.8 21.0 %all-gather.7.cloned.1.call-done = bf16[512,2048]{1,0:T(8,128)(2,1)} async-done(((bf16[128,2048]{1,0:T(8,128)(2,1)}), bf16[512,2048]{1,0:T(8,128)(2,1)}) %all-gather.7.cloned.1.call-update) | async-done | bytes 2097168 | tf_op jit(solution)/shard_map/all_gather | solution.py:102
  71.9 21.5 %reduce-scatter.5.cloned.1.call-done = bf16[128,2048]{1,0:T(8,128)(2,1)} async-done(((bf16[512,2048]{1,0:T(8,128)(2,1)}), bf16[128,2048]{1,0:T(8,128)(2,1)}) %reduce-scatter.5.cloned.1.call-update) | async-done | bytes 524304 | tf_op jit(solution)/shard_map/reduce_scatter | solution.py:149
  101.8 87.5 %all_to_all.66 = bf16[16,56,2048]{2,1,0:T(8,128)(2,1)S(1)} all-to-all(bf16[16,56,2048]{2,1,0:T(8,128)(2,1)} %bitcast.165), channel_id=1, replica_groups=mesh['exp'=8,'tp'=4] {'exp'}, dimensions={0} | all-to-all | bytes 7340032 | tf_op jit(solution)/shard_map/all_to_all | solution.py:177
  197.7 12.3 gather_fusion.2
  210.1 85.0 %all_to_all.67 = bf16[16,56,2048]{2,1,0:T(8,128)(2,1)S(1)} all-to-all(bf16[16,56,2048]{2,1,0:T(8,128)(2,1)} %bitcast.166), channel_id=1, replica_groups=mesh['exp'=8,'tp'=4] {'exp'}, dimensions={0} | all-to-all | bytes 7340032 | tf_op jit(solution)/shard_map/all_to_all | solution.py:206
  297.5 13.5 fusion.53
  320.8 68.7 %all-gather.11.cloned.1.call-done = bf16[2,1792,2048]{2,1,0:T(8,128)(2,1)} async-done(((bf16[2,448,2048]{2,1,0:T(8,128)(2,1)}), bf16[2,1792,2048]{2,1,0:T(8,128)(2,1)}) %all-gather.11.cloned.1.call-update) | async-done | bytes 14680080 | tf_op jit(solution)/shard_map/all_gather | solution.py:207
  389.5 15.6 %multiply_convert_fusion.1 = (bf16[2,1792,256]{2,1,0:T(8,128)(2,1)}, bf16[2,1792,256]{2,1,0:T(8,128)(2,1)}, bf16[2,1792,256]{2,1,0:T(8,128)(2,1)}) fusion(f32[2,1792,256]{2,1,0:T(8,128)} %fusion.52, f32[2,1792,256]{2,1,0:T(8,128)} %fusion.53, bf16[2,1792,2048]{2,1,0:T(8,128)(2,1)} %all-gather.11.cloned.1.call-done, bf16[2,256,2048]{2,1,0:T(8,128)(2,1)S(1)} %copy-done), kind=kOutput, calls=%fused_computation.22 | convolution fusion | flops 3771858944 | bytes 29622272 | tf_op jit(solution)/shard_map/erd,efd->erf/dot_general | solution.py:215
  415.4 19.2 %fusion.54 = f32[2,1792,2048]{2,1,0:T(8,128)} fusion(bf16[2,1792,256]{2,1,0:T(8,128)(2,1)} %get-tuple-element.32, bf16[2,2048,256]{2,1,0:T(8,128)(2,1)S(1)} %copy-done.34), kind=kOutput, calls=%fused_computation.160 | convolution fusion | flops 3758096384 | bytes 33292288 | tf_op jit(solution)/shard_map/erf,edf->erd/dot_general | solution.py:227
  434.6 17.7 %add_convert_fusion = bf16[2,1792,2048]{2,1,0:T(8,128)(2,1)} fusion(f32[2,1792,2048]{2,1,0:T(8,128)} %fusion.54, bf16[2,1792,256]{2,1,0:T(8,128)(2,1)S(1)} %copy-done.42, bf16[2,2048,256]{2,1,0:T(8,128)(2,1)S(1)} %copy-done.35), kind=kOutput, calls=%fused_computation.5 | convolution fusion | flops 3772776448 | bytes 47972352 | tf_op jit(solution)/shard_map/erf,edf->erd/dot_general | solution.py:229
  452.3 74.5 %reduce-scatter.7.cloned.1.call-done = bf16[2,448,2048]{2,1,0:T(8,128)(2,1)} async-done(((bf16[2,1792,2048]{2,1,0:T(8,128)(2,1)}), bf16[2,448,2048]{2,1,0:T(8,128)(2,1)}) %reduce-scatter.7.cloned.1.call-update) | async-done | bytes 3670032 | tf_op jit(solution)/shard_map/reduce_scatter | solution.py:187
  539.9 102.3 %reduce-scatter.9.cloned.1.call-done = bf16[2,448,2048]{2,1,0:T(8,128)(2,1)} async-done(((bf16[2,1792,2048]{2,1,0:T(8,128)(2,1)}), bf16[2,448,2048]{2,1,0:T(8,128)(2,1)}) %reduce-scatter.9.cloned.1.call-update) | async-done | bytes 3670032 | tf_op jit(solution)/shard_map/reduce_scatter | solution.py:230
  661.9 11.3 gather_fusion.1
  679.2 58.3 %all-to-all-done.3 = bf16[2,448,2048]{2,0,1:T(2,128)(2,1)} async-done(((bf16[2,448,2048]{2,0,1:T(2,128)(2,1)}), bf16[2,448,2048]{2,0,1:T(2,128)(2,1)}, u32[]{:S(2)}, u32[]{:S(2)}) %all-to-all-start.3) | async-done | bytes 3670048 | tf_op jit(solution)/shard_map/all_to_all | solution.py:233
  743.5 11.3 gather_fusion.3
  762.6 20.6 %all-gather.13.cloned.1.call-done = bf16[512,2048]{1,0:T(8,128)(2,1)} async-done(((bf16[128,2048]{1,0:T(8,128)(2,1)}), bf16[512,2048]{1,0:T(8,128)(2,1)}) %all-gather.13.cloned.1.call-update) | async-done | bytes 2097168 | tf_op jit(solution)/shard_map/all_gather | solution.py:249
  827.5 11.3 fusion.58
  838.9 11.0 fusion.57
  856.7 22.3 %all-reduce.5 = (bf16[512]{0:T(512)(128)(2,1)S(1)}, bf16[512]{0:T(512)(128)(2,1)S(1)}) all-reduce(bf16[512]{0:T(512)(128)(2,1)S(1)} %get-tuple-element.36, bf16[512]{0:T(512)(128)(2,1)S(1)} %get-tuple-element.34), channel_id=1, replica_groups=mesh['exp'=8,'tp'=4] {'exp'}, use_global_device_ids=true, to_apply=%region_35.36 | all-reduce | flops 1024 | bytes 4096 | tf_op jit(solution)/shard_map/psum | solution.py:311
  885.0 40.7 %all-reduce.4 = (f32[2048]{0:T(1024)}, f32[2048]{0:T(1024)}) all-reduce(f32[2048]{0:T(1024)S(1)} %get-tuple-element.18, f32[2048]{0:T(1024)S(1)} %get-tuple-element.16), channel_id=1, replica_groups=mesh['exp'=8,'tp'=4] {'exp','tp'}, use_global_device_ids=true, to_apply=%region_29.30 | all-reduce | flops 4096 | bytes 32768 | tf_op jit(solution)/shard_map/psum | solution.py:314
  925.6 137.9 %all-reduce.12.cloned.1.call-done = (bf16[2048,512]{1,0:T(8,128)(2,1)}, bf16[2048,512]{1,0:T(8,128)(2,1)}, bf16[512,2048]{1,0:T(8,128)(2,1)}) async-done(((bf16[2048,512]{1,0:T(8,128)(2,1)}, bf16[2048,512]{1,0:T(8,128)(2,1)}, bf16[512,2048]{1,0:T(8,128)(2,1)}), (bf16[2048,512]{1,0:T(8,128)(2,1)}, bf16[2048,512]{1,0:T(8,128)(2,1)}, bf16[512,2048]{1,0:T(8,128)(2,1)})) %all-reduce.12.cloned.1.call-update) | async-done | bytes 6291472 | tf_op jit(solution)/shard_map/psum | solution.py:308
  1073.0 219.8 %all-gather.15.cloned.1.call-done = bf16[16384,512]{1,0:T(8,128)(2,1)} async-done(((bf16[2048,512]{1,0:T(8,128)(2,1)}), bf16[16384,512]{1,0:T(8,128)(2,1)}) %all-gather.15.cloned.1.call-update) | async-done | bytes 16777232 | tf_op jit(solution)/shard_map/all_gather | solution.py:15
  1292.9 10.7 reduce_sum.239
  1307.8 112.8 %all-reduce.10.cloned.1.call-done = f32[2048,16]{0,1:T(8,128)} async-done(((f32[2048,16]{0,1:T(8,128)}), f32[2048,16]{0,1:T(8,128)}) %all-reduce.10.cloned.1.call-update) | async-done | bytes 131088 | tf_op jit(solution)/shard_map/psum | solution.py:314
  (295 shorter events, 206.9 us)
Async XLA Ops:
  7.2 382.3 %copy-start = (bf16[2,256,2048]{2,1,0:T(8,128)(2,1)S(1)}, bf16[2,256,2048]{2,1,0:T(8,128)(2,1)}, u32[]{:S(2)}) copy-start(bf16[2,256,2048]{2,1,0:T(8,128)(2,1)} %param.29) | copy-start | bytes 6291460
  7.2 29.5 %all-gather.7.cloned.1.call-start = ((), (), s32[]{:S(2)}) async-start(), calls=%async_computation.8 | async-start | bytes 2621440 | tf_op jit(solution)/shard_map/all_gather | solution.py:102
  11.3 82.1 %reduce-scatter.5.cloned.1.call-start = ((), (), s32[]{:S(2)}) async-start(), calls=%async_computation.9 | async-start | bytes 2621440 | tf_op jit(solution)/shard_map/reduce_scatter | solution.py:149
  15.8 34.2 %copy-start.31 = (f32[512,64]{1,0:T(8,128)}, f32[512,64]{1,0:T(8,128)S(1)}, u32[]{:S(2)}) copy-start(f32[512,64]{1,0:T(8,128)S(1)} %get-tuple-element.56) | copy-start | bytes 393220
  59.1 34.3 %copy-start.4 = (bf16[128,2048]{1,0:T(8,128)(2,1)S(1)}, bf16[128,2048]{1,0:T(8,128)(2,1)}, u32[]{:S(2)}) copy-start(bf16[128,2048]{1,0:T(8,128)(2,1)} %param.16) | copy-start | bytes 1572868
  59.1 35.6 %copy-start.49 = (f32[2048]{0:T(1024)S(1)}, f32[2048]{0:T(1024)}, u32[]{:S(2)}) copy-start(f32[2048]{0:T(1024)} %param.25) | copy-start | bytes 24580
  61.7 235.7 %all-gather.9.cloned.1.call-start = ((), (), s32[]{:S(2)}) async-start(), calls=%async_computation.10 | async-start | bytes 18350080 | tf_op jit(solution)/shard_map/all_gather | solution.py:70
  191.5 197.9 %all-gather.11.cloned.1.call-start = ((), (), s32[]{:S(2)}) async-start(), calls=%async_computation.12 | async-start | bytes 18350080 | tf_op jit(solution)/shard_map/all_gather | solution.py:207
  297.4 229.4 %reduce-scatter.7.cloned.1.call-start = ((), (), s32[]{:S(2)}) async-start(), calls=%async_computation.11 | async-start | bytes 18350080 | tf_op jit(solution)/shard_map/reduce_scatter | solution.py:187
  413.8 228.5 %reduce-scatter.9.cloned.1.call-start = ((), (), s32[]{:S(2)}) async-start(), calls=%async_computation.13 | async-start | bytes 18350080 | tf_op jit(solution)/shard_map/reduce_scatter | solution.py:230
  415.4 19.2 %copy-start.42 = (bf16[2,1792,256]{2,1,0:T(8,128)(2,1)S(1)}, bf16[2,1792,256]{2,1,0:T(8,128)(2,1)}, u32[]{:S(2)}) copy-start(bf16[2,1792,256]{2,1,0:T(8,128)(2,1)} %get-tuple-element.31) | copy-start | bytes 5505028
  534.4 115.5 %all-to-all-start.1 = ((bf16[2,448,2048]{2,0,1:T(2,128)(2,1)}), bf16[2,448,2048]{2,0,1:T(2,128)(2,1)}, u32[]{:S(2)}, u32[]{:S(2)}) async-start(bf16[2,448,2048]{2,0,1:T(2,128)(2,1)} %copy.151), calls=%async_computation.3 | async-start | bytes 7340032 | tf_op jit(solution)/shard_map/all_to_all | solution.py:190
  649.9 87.6 %all-to-all-start.3 = ((bf16[2,448,2048]{2,0,1:T(2,128)(2,1)}), bf16[2,448,2048]{2,0,1:T(2,128)(2,1)}, u32[]{:S(2)}, u32[]{:S(2)}) async-start(bf16[2,448,2048]{2,0,1:T(2,128)(2,1)} %copy.155), calls=%async_computation.6 | async-start | bytes 7340032 | tf_op jit(solution)/shard_map/all_to_all | solution.py:233
  655.4 127.8 %all-gather.13.cloned.1.call-start = ((), (), s32[]{:S(2)}) async-start(), calls=%async_computation.14 | async-start | bytes 2621440 | tf_op jit(solution)/shard_map/all_gather | solution.py:249
  762.3 117.8 %reduce-scatter.11.cloned.1.call-start = ((), (), s32[]{:S(2)}) async-start(), calls=%async_computation.15 | async-start | bytes 2621440 | tf_op jit(solution)/shard_map/reduce_scatter | solution.py:296
  812.4 251.1 %all-reduce.12.cloned.1.call-start = ((), (), s32[]{:S(2)}) async-start(), calls=%async_computation.18 | async-start | bytes 12582912 | tf_op jit(solution)/shard_map/psum | solution.py:308
  822.2 470.7 %all-gather.15.cloned.1.call-start = ((), (), s32[]{:S(2)}) async-start(), calls=%async_computation.17 | async-start | bytes 18874368 | tf_op jit(solution)/shard_map/all_gather | solution.py:15
  827.5 593.1 %all-reduce.10.cloned.1.call-start = ((), (), s32[]{:S(2)}) async-start(), calls=%async_computation.16 | async-start | bytes 262144 | tf_op jit(solution)/shard_map/psum | solution.py:314
  827.5 22.4 %slice-start = ((s8[14680064]{0:T(1024)(128)(4,1)}), s8[4194304]{0:T(1024)(128)(4,1)S(1)}, s32[]{:S(2)}) async-start(s8[14680064]{0:T(1024)(128)(4,1)} %bitcast.162), calls=%async_computation.19 | async-start | bytes 8388608
  827.5 22.4 %slice-start.1 = ((s8[14680064]{0:T(1024)(128)(4,1)}), s8[4194304]{0:T(1024)(128)(4,1)S(1)}, s32[]{:S(2)}) async-start(s8[14680064]{0:T(1024)(128)(4,1)} %bitcast.162), calls=%async_computation.20 | async-start | bytes 8388608
  850.0 30.2 %copy-start.55 = (f32[2048]{0:T(1024)S(1)}, f32[2048]{0:T(1024)}, u32[]{:S(2)}) copy-start(f32[2048]{0:T(1024)} %param.18) | copy-start | bytes 24580
  850.0 30.2 %copy-start.68 = (f32[128]{0:T(128)S(1)}, f32[128]{0:T(128)}, u32[]{:S(2)}) copy-start(f32[128]{0:T(128)} %copy-done.67) | copy-start | bytes 1540
  850.0 31.7 %copy-start.14 = (bf16[128,2048]{1,0:T(8,128)(2,1)S(1)}, bf16[128,2048]{1,0:T(8,128)(2,1)}, u32[]{:S(2)}) copy-start(bf16[128,2048]{1,0:T(8,128)(2,1)} %param.17) | copy-start | bytes 1572868
  1292.9 129.2 %copy-start.1 = (bf16[2,256,2048]{2,1,0:T(8,128)(2,1)S(1)}, bf16[2,256,2048]{2,1,0:T(8,128)(2,1)}, u32[]{:S(2)}) copy-start(bf16[2,256,2048]{2,1,0:T(8,128)(2,1)} %param.29) | copy-start | bytes 6291460
  (67 other events, 252.1 us)
Sparse Core Ops, SparseCore 0:
  11.4 25.2 all-gather.6
  61.9 31.4 reduce-scatter.4
  191.7 92.0 all-gather.8
  297.5 91.9 all-gather.10
  413.9 112.8 reduce-scatter.6
  529.4 112.8 reduce-scatter.8
  762.5 20.7 all-gather.12
  812.6 31.4 reduce-scatter.10
  848.9 214.5 all-reduce.11
  1066.3 226.5 all-gather.14
  1299.9 120.5 all-reduce.9
